TPU v7x, 256 devices: a whole 4x4x8 slice. The times are simulated.
256 devices in a mesh: cls: 32 (over z, x), pb: 8 (over y, core).
Axes of the slice: x: 4, y: 4, z: 8, core: 2. Of those that a mesh axis runs over, the one named last changes fastest.
Arguments:
- queries: bfloat16 [4096, 1024], P('pb'), may hold values from -40 to 40
- labels: int32 [4096], replicated, may hold values from 0 to 98303
- prototypes: bfloat16 [98304, 1024], P('cls'), may hold values from -8 to 8
Outputs:
- query_loss: float32 [4096], P('pb')
- query_grad: float32 [4096, 1024], P('pb')
- proto_grad: float32 [98304, 1024], P(('cls', 'pb'))
All inputs are finite; a program needn't handle non-finite values.
Results may differ from a plain program's by a relative error of at most 0.0012.
Values may be sent and summed in bfloat16 or wider, within the bound.
A program may use at most 128 MiB of HBM per device.

v0:
```python
import math

import jax
import jax.numpy as jnp
from jax import lax
from jax.sharding import PartitionSpec as P


def copy_for_each(value, axis):
    size = lax.axis_size(axis)
    return lax.all_to_all(
        jnp.broadcast_to(value[None], (size, *value.shape)), axis, 0, 0, tiled=True
    )


def gathered_once(value, axis):
    leaves = jax.tree.leaves(value)
    order = sorted(range(len(leaves)), key=lambda k: -leaves[k].size)
    width = (1, *leaves[order[0]].shape)[-1]
    lines = [
        jnp.pad(leaves[k].reshape(-1), (0, -leaves[k].size % width)).reshape(-1, width)
        for k in order
    ]
    both, at, found = (copy_for_each(jnp.concatenate(lines), axis), 0, {})
    for k, line in zip(order, lines):
        piece = both[:, at : at + len(line)].reshape(len(both), -1)
        found[k] = piece[:, : leaves[k].size].reshape(-1, *leaves[k].shape)
        at += len(line)
    numbers = iter(range(len(leaves)))
    return jax.tree.map(lambda _: found[next(numbers)], value)


def joined_by_halves(pieces, combine):
    while len(jax.tree.leaves(pieces)[0]) > 1:
        pieces = jax.vmap(combine)(
            *(jax.tree.map(lambda part: part[side::2], pieces) for side in (0, 1))
        )
    return jax.tree.map(lambda part: part[0], pieces)


def joined_all(value, axis, combine):
    pieces = gathered_once(value, axis)
    return joined_by_halves(pieces, combine)


def rows_for(lines, size):
    spare = -lines.shape[0] % size
    if not spare:
        return lines
    return jnp.concatenate([lines, jnp.zeros((spare, *lines.shape[1:]), lines.dtype)])


def laid_out(parts, dim):
    parts = jnp.moveaxis(parts, 0, dim)
    dims = parts.shape
    return parts.reshape(*dims[:dim], dims[dim] * dims[dim + 1], *dims[dim + 2 :])


def collect(value, axis, dim):
    return laid_out(copy_for_each(value, axis), dim)


def cut_along(value, dim, size):
    dims = value.shape
    parts = value.reshape(*dims[:dim], size, dims[dim] // size, *dims[dim + 1 :])
    return jnp.moveaxis(parts, dim, 0)


def sum_at_owner(value, axis, dim):
    parts = cut_along(value, dim, lax.axis_size(axis))
    arrived = lax.all_to_all(parts, axis, split_axis=0, concat_axis=0, tiled=True)
    return arrived.sum(axis=0)


def total_of(value, axes):
    lines = value.reshape(-1, value.shape[-1])
    padded = rows_for(lines, lax.axis_size(axes))
    whole = collect(sum_at_owner(padded, axes, 0), axes, 0)
    return lax.slice_in_dim(whole, 0, len(lines)).reshape(value.shape)


def combine_rows(earlier, latter):
    row_top = jnp.maximum(earlier[0], latter[0])
    row_total = earlier[1] * jnp.exp(earlier[0] - row_top) + latter[1] * jnp.exp(
        latter[0] - row_top
    )
    return (row_top, row_total, earlier[2] + latter[2])


def local(queries, labels, prototypes):
    factor = 1.0 / math.sqrt(queries.shape[1])
    class_rows = prototypes.shape[0]
    query_count = queries.shape[0]
    batch_start = lax.axis_index("pb") * query_count
    first_class = lax.axis_index("cls") * class_rows
    my_labels = lax.dynamic_slice_in_dim(labels, batch_start, query_count, 0)
    proto_float = prototypes.astype(jnp.float32)
    proto_norm = jnp.sum(proto_float * proto_float, axis=1)
    query_float = queries.astype(jnp.float32)
    query_norm = jnp.sum(query_float * query_float, axis=1)
    inner_block = lax.dot_general(
        queries, prototypes, (((1,), (1,)), ((), ())), preferred_element_type=jnp.float32
    )
    logits = factor * (2.0 * inner_block - proto_norm[None, :] - query_norm[:, None])
    columns = first_class + lax.iota(jnp.int32, class_rows)
    label_mask = my_labels[:, None] == columns[None, :]
    local_top = jnp.max(logits, axis=1)
    local_total = jnp.sum(jnp.exp(logits - local_top[:, None]), axis=1)
    label_part = jnp.sum(jnp.where(label_mask, logits, 0.0), axis=1)
    row_top, row_total, label_logit = joined_all(
        (local_top, local_total, label_part), "cls", combine_rows
    )
    log_total = row_top + jnp.log(row_total)
    query_loss = log_total - label_logit
    grad_logit = (jnp.exp(logits - log_total[:, None]) - label_mask.astype(jnp.float32)).astype(
        jnp.bfloat16
    )
    query_term = jnp.dot(grad_logit, prototypes, preferred_element_type=jnp.float32)
    query_grad = 2.0 * factor * total_of(query_term, "cls")
    col_partial = jnp.sum(grad_logit.astype(jnp.float32), axis=0)
    moment_part = lax.dot_general(
        grad_logit, queries, (((0,), (0,)), ((), ())), preferred_element_type=jnp.float32
    )
    proto_grad = lax.psum_scatter(
        2.0 * factor * (moment_part - col_partial[:, None] * proto_float),
        "pb",
        scatter_dimension=0,
        tiled=True,
    )
    return (query_loss, query_grad, proto_grad)


def solution(mesh):
    placed = (P("pb", None), P(), P("cls", None))
    return jax.shard_map(
        local,
        mesh=mesh,
        in_specs=placed,
        out_specs=(P("pb"), P("pb", None), P(("cls", "pb"), None)),
        check_vma=False,
    )
```

profile of v0, /device:TPU:24, one launch (start us, length us, event | category | flops | bytes accessed | tf_op | source)
XLA Modules:
  0.0 185.8 jit_solution(7258799466327150755)
XLA Ops:
  7.2 0.0 copy-start.3
  7.2 0.0 reduce-scatter.2.cloned.1.call-start
  7.2 4.2 %fusion = f32[3072]{0:T(1024)S(1)} fusion(bf16[3072,1024]{1,0:T(8,128)(2,1)} %param.5), kind=kLoop, calls=%fused_computation.2 | loop fusion | flops 9434112 | bytes 6303744 | tf_op jit(solution)/shard_map/reduce_sum | solution.py:98
  11.4 0.0 copy-done.3
  11.4 0.3 multiply_reduce_fusion
  11.7 0.8 dynamic_slice.3
  12.5 6.0 %fusion.10 = (f32[512]{0:T(512)S(1)}, f32[512,3072]{1,0:T(8,128)S(1)}) fusion(f32[512]{0:T(512)S(1)} %multiply_reduce_fusion, f32[3072]{0:T(1024)S(1)} %fusion, bf16[512,1024]{1,0:T(8,128)(2,1)S(1)} %copy-done.3, bf16[3072,1024]{1,0:T(8,128)(2,1)} %param.5), kind=kOutput, calls=%fused_computation.32 | convolution fusion | flops 3229089280 | bytes 13647872 | tf_op jit(solution)/shard_map/dot_general | solution.py:101
  18.5 0.0 copy-start
  18.5 2.7 %copy-done = f32[512,3072]{1,0:T(8,128)} copy-done((f32[512,3072]{1,0:T(8,128)}, f32[512,3072]{1,0:T(8,128)S(1)}, u32[]{:S(2)}) %copy-start) | copy-done | bytes 6291480
  21.1 1.9 %exponential_reduce_fusion = (f32[512]{0:T(512)S(1)}, f32[512]{0:T(512)S(1)}) fusion(f32[512,3072]{1,0:T(8,128)S(1)} %get-tuple-element.19, f32[512]{0:T(512)S(1)} %get-tuple-element.18, s32[3072]{0:T(1024)S(1)} %iota_add_fusion, s32[512]{0:T(512)S(1)} %dynamic_slice.3), kind=kLoop, calls=%fused_computation.11 | loop fusion | flops 7863296 | bytes 6311936 | tf_op jit(solution)/shard_map/reduce_sum | solution.py:108
  23.0 0.0 slice-start
  23.1 23.9 %all_to_all.15 = f32[32,3,512]{2,1,0:T(4,128)S(1)} all-to-all(f32[32,3,512]{2,1,0:T(4,128)S(1)} %broadcast_in_dim.9), channel_id=1, replica_groups=mesh['cls'=32,'pb'=8] {'cls'}, dimensions={0} | all-to-all | bytes 393216 | tf_op jit(solution)/shard_map/all_to_all | solution.py:11
  47.1 0.1 fusion.9
  47.7 0.0 slice-start.1
  47.7 3.9 %convert_reduce_fusion = (f32[3072]{0:T(1024)S(1)}, bf16[512,3072]{1,0:T(8,128)(2,1)S(1)}) fusion(s32[3072]{0:T(1024)S(1)} %iota_add_fusion, s32[512]{0:T(512)S(1)} %dynamic_slice.3, f32[512,3072]{1,0:T(8,128)} %copy-done, f32[512]{0:T(512)S(1)} %bitcast.26), kind=kLoop, calls=%fused_computation.10 | loop fusion | flops 11006976 | bytes 9465856 | tf_op jit(solution)/shard_map/reduce_sum | solution.py:120
  51.7 0.0 copy-start.1
  51.7 1.7 copy-done.1
  53.3 0.0 slice-done
  53.4 0.0 slice-done.1
  53.4 7.0 %fusion.2 = f32[3072,1024]{1,0:T(8,128)} fusion(bf16[3072,1024]{1,0:T(8,128)(2,1)S(1)} %bitcast.21, f32[3072]{0:T(1024)S(1)} %get-tuple-element.5, bf16[512,3072]{1,0:T(8,128)(2,1)S(1)} %get-tuple-element.6, bf16[512,1024]{1,0:T(8,128)(2,1)S(1)} %copy-done.3), kind=kOutput, calls=%fused_computation.4 | convolution fusion | flops 3233808384 | bytes 23080960 | tf_op jit(solution)/shard_map/dot_general | solution.py:121
  60.4 0.0 copy-start.2
  60.4 0.0 reduce-scatter.2.cloned.1.call-update
  60.4 1.9 %copy-done.2 = bf16[512,3072]{1,0:T(8,128)(2,1)S(1)} copy-done((bf16[512,3072]{1,0:T(8,128)(2,1)S(1)}, bf16[512,3072]{1,0:T(8,128)(2,1)}, u32[]{:S(2)}) %copy-start.2) | copy-done | bytes 3145752
  62.3 5.5 %fusion.11 = f32[512,1024]{1,0:T(8,128)S(1)} fusion(bf16[512,3072]{1,0:T(8,128)(2,1)S(1)} %copy-done.2, bf16[3072,1024]{1,0:T(8,128)(2,1)} %param.5), kind=kOutput, calls=%fused_computation.33 | convolution fusion | flops 3221225472 | bytes 11534336 | tf_op jit(solution)/shard_map/dot_general | solution.py:118
  67.7 53.6 %all_to_all.16 = f32[32,16,1024]{2,1,0:T(8,128)S(1)} all-to-all(f32[32,16,1024]{2,1,0:T(8,128)S(1)} %bitcast.23), channel_id=1, replica_groups=mesh['cls'=32,'pb'=8] {'cls'}, dimensions={0} | all-to-all | bytes 4194304 | tf_op jit(solution)/shard_map/all_to_all | solution.py:71
  121.3 0.1 reduce_sum.58
  121.4 1.6 broadcast_in_dim.10
  123.0 5.6 %all-to-all-start.2 = ((f32[32,16,1024]{2,1,0:T(8,128)}), f32[32,16,1024]{2,1,0:T(8,128)S(1)}, u32[]{:S(2)}, u32[]{:S(2)}) async-start(f32[32,16,1024]{2,1,0:T(8,128)} %broadcast_in_dim.10), calls=%async_computation.2 | async-start | bytes 4194304 | tf_op jit(solution)/shard_map/all_to_all | solution.py:11
  128.8 0.6 sub.87
  129.4 48.0 %all-to-all-done.2 = f32[32,16,1024]{2,1,0:T(8,128)S(1)} async-done(((f32[32,16,1024]{2,1,0:T(8,128)}), f32[32,16,1024]{2,1,0:T(8,128)S(1)}, u32[]{:S(2)}, u32[]{:S(2)}) %all-to-all-start.2) | async-done | bytes 2097184 | tf_op jit(solution)/shard_map/all_to_all | solution.py:11
  177.4 1.5 broadcast_multiply_fusion
  178.9 0.0 reduce-scatter.2.cloned.1.call-done
  (40 shorter events, 0.7 us)
Async XLA Ops:
  7.2 4.2 %copy-start.3 = (bf16[512,1024]{1,0:T(8,128)(2,1)S(1)}, bf16[512,1024]{1,0:T(8,128)(2,1)}, u32[]{:S(2)}) copy-start(bf16[512,1024]{1,0:T(8,128)(2,1)} %param.3) | copy-start | bytes 3145732
  7.2 171.7 %reduce-scatter.2.cloned.1.call-start = ((), (), s32[]{:S(2)}) async-start(), calls=%async_computation.4 | async-start | bytes 14155776 | tf_op jit(solution)/shard_map/reduce_scatter | solution.py:124
  18.5 2.7 %copy-start = (f32[512,3072]{1,0:T(8,128)}, f32[512,3072]{1,0:T(8,128)S(1)}, u32[]{:S(2)}) copy-start(f32[512,3072]{1,0:T(8,128)S(1)} %get-tuple-element.19) | copy-start | bytes 18874372
  23.0 30.3 %slice-start = ((s8[6291456]{0:T(1024)(128)(4,1)}), s8[2097152]{0:T(1024)(128)(4,1)S(1)}, s32[]{:S(2)}) async-start(s8[6291456]{0:T(1024)(128)(4,1)} %bitcast.20), calls=%async_computation.5 | async-start | bytes 4194304
  47.7 5.6 %slice-start.1 = ((s8[6291456]{0:T(1024)(128)(4,1)}), s8[4194304]{0:T(1024)(128)(4,1)S(1)}, s32[]{:S(2)}) async-start(s8[6291456]{0:T(1024)(128)(4,1)} %bitcast.20), calls=%async_computation.6 | async-start | bytes 8388608
  51.7 1.7 copy-start.1
  60.4 1.9 %copy-start.2 = (bf16[512,3072]{1,0:T(8,128)(2,1)S(1)}, bf16[512,3072]{1,0:T(8,128)(2,1)}, u32[]{:S(2)}) copy-start(bf16[512,3072]{1,0:T(8,128)(2,1)} %copy-done.1) | copy-start | bytes 9437188
  123.0 54.4 %all-to-all-start.2 = ((f32[32,16,1024]{2,1,0:T(8,128)}), f32[32,16,1024]{2,1,0:T(8,128)S(1)}, u32[]{:S(2)}, u32[]{:S(2)}) async-start(f32[32,16,1024]{2,1,0:T(8,128)} %broadcast_in_dim.10), calls=%async_computation.2 | async-start | bytes 4194304 | tf_op jit(solution)/shard_map/all_to_all | solution.py:11
Sparse Core Ops, SparseCore 0:
  60.5 68.5 reduce-scatter.1
where the time goes:
time: 187 us; the launch traced here: 186 us
  blocking collectives  77.5 us (41%)
  waiting for transfers between devices  48 us (26%)
  matrix products  18.5 us (10%)
  between operations  14.2 us (8%)
  other arithmetic  12.6 us (7%)
  local copies, waits for them, and re-layouts  9.22 us (5%)
  starting transfers between devices  5.63 us (3%)
    all_to_all x1, blocking collectives, sum_at_owner(): lax.all_to_all(parts, axis, split_axis=0, concat_axis=0, tiled=True)  53.6 us
    all_to_all x1, waiting for transfers between devices, copy_for_each(): lax.all_to_all(jnp.broadcast_to(value[None], (size, *value.shape)), axis,...  48 us
    all_to_all x1, blocking collectives, copy_for_each(): lax.all_to_all(jnp.broadcast_to(value[None], (size, *value.shape)), axis,...  23.9 us
    dot_general x1, matrix products, local(): lax.dot_general(grad_logit, queries, (((0,), (0,)), ((), ())), preferred_...  7.01 us
    unnamed x13, local copies, waits for them, and re-layouts  6.21 us
    dot_general x1, matrix products, local(): lax.dot_general(queries, prototypes, (((1,), (1,)), ((), ())), preferred_...  6.01 us
    all_to_all x1, starting transfers between devices, copy_for_each(): lax.all_to_all(jnp.broadcast_to(value[None], (size, *value.shape)), axis,...  5.59 us
    dot_general x1, matrix products, local(): jnp.dot(grad_logit, prototypes, preferred_element_type=jnp.float32)  5.48 us
  transfers between devices with their start and end apart: 2, of which 1 were waited for; matrix products, arithmetic and copies ran while one was open for 5% of the time, Pallas kernels for 0%

commit v1 on v0

v1 whole, which is shorter than its diff:
```python
import math

import jax
import jax.numpy as jnp
from jax import lax
from jax.experimental import pallas as pl
from jax.experimental.pallas import tpu as pltpu
from jax.sharding import PartitionSpec as P

MESH = pl.DeviceIdType.MESH
NX, NZ, NY = 4, 8, 4
PARTS = 2
TOP = 32000.0

NT = (((1,), (1,)), ((), ()))
NN = (((1,), (0,)), ((), ()))
SLOTS = ((0, 0), (0, 1), (3, 0), (1, 0), (3, 1), (1, 1), (2, 0), (2, 1))


def dot(a, b, dims):
    return lax.dot_general(a, b, dims, preferred_element_type=jnp.float32)


def coded(value):
    top = jnp.max(jnp.abs(value), axis=0, keepdims=True)
    power = jnp.ceil(jnp.log2(jnp.maximum(top, 1e-30)) + 1e-4)
    lines = jnp.round(value * (jnp.exp2(-power) * TOP))
    lines = jnp.clip(lines, -32767.0, 32767.0)
    lines = lines.astype(jnp.int32).astype(jnp.int16)
    return lines, jnp.broadcast_to(power, (16, power.shape[1])).astype(jnp.int32).astype(jnp.int16)


def scale_of(power):
    return jnp.exp2(power.astype(jnp.float32)) * (1.0 / TOP)


def lanes_of(tile, first):
    return jnp.concatenate([tile[first + k : first + k + 1] for k in range(4)], axis=1)


def rows_of(line):
    return jnp.concatenate([line[:, 128 * k : 128 * k + 128] for k in range(4)], axis=0)


def kernel(
    q_in, labels, p_in, loss_out, qg_out, pg_out,
    protos, qall, logits, grad, pn_line, own_x, stat_x, stat_z, row_line,
    lab_col, m_col, tot_col, lbl_col, w_col,
    xs, xr, zs, zr, zown, gx, acc, coltot, pn_own,
    in_sem, q_ssem, q_rsem, st_ssem, st_rsem, pb_ssem, pb_rsem,
    x_ssem, x_rsem, z_ssem, z_rsem, gz_ssem, gz_rsem, gx_ssem, gx_rsem,
):
    ci, pi = lax.axis_index("cls"), lax.axis_index("pb")
    z, x, y, core = ci // NX, lax.rem(ci, NX), pi // 2, lax.rem(pi, 2)
    queries, width = q_in.shape
    classes = p_in.shape[0]
    own_rows = pg_out.shape[0]
    factor = 1.0 / math.sqrt(width)
    block = queries // NX
    part = block // PARTS
    first_class = ci * classes

    def at_x(d):
        return lax.rem(x + d, NX)

    def at_z(d):
        return lax.rem(z + d, NZ)

    def dev_x(d):
        return (z * NX + at_x(d), pi)

    def dev_z(d):
        return (at_z(d) * NX + x, pi)

    def dev_pb(dy, other):
        return (ci, lax.rem(y + dy, NY) * 2 + lax.rem(core + other, 2))

    def pb_of(slot):
        dy, other = SLOTS[slot]
        return lax.rem(y + dy, NY) * 2 + lax.rem(core + other, 2)

    def send(src, dst, ssem, rsem, dev):
        copy = pltpu.make_async_remote_copy(
            src_ref=src, dst_ref=dst, send_sem=ssem, recv_sem=rsem, device_id=dev, device_id_type=MESH
        )
        copy.start()
        return copy

    def arrived(ref, ssem, rsem):
        pltpu.make_async_remote_copy(
            src_ref=ref, dst_ref=ref, send_sem=ssem, recv_sem=rsem, device_id=(ci, pi), device_id_type=MESH
        ).wait_recv()

    sent = []

    chunk = 512
    chunks = classes // chunk
    q_load = pltpu.make_async_copy(q_in, qall.at[0], in_sem.at[chunks])
    q_load.start()
    p_loads = [
        pltpu.make_async_copy(p_in.at[pl.ds(k * chunk, chunk)], protos.at[pl.ds(k * chunk, chunk)], in_sem.at[k])
        for k in range(chunks)
    ]
    for load in p_loads:
        load.start()

    barrier = pltpu.get_barrier_semaphore()
    peers = [dev_x(d) for d in range(1, NX)] + [dev_z(d) for d in range(1, NZ)]
    peers += [dev_pb(dy, o) for dy in range(NY) for o in range(2) if dy or o]
    for dev in peers:
        pl.semaphore_signal(barrier, inc=1, device_id=dev, device_id_type=MESH)

    q_load.wait()
    my_label = lanes_of(labels[pi], 0)
    lab_col[...] = jnp.broadcast_to(my_label - first_class, (128, queries)).T

    for k in range(queries // 128):
        q32 = qall[0, pl.ds(k * 128, 128), :].astype(jnp.float32)
        q32 = q32 * q32
        part_sum = sum(q32[:, 128 * i : 128 * i + 128] for i in range(width // 128))
        row_line[1:2, 128 * k : 128 * k + 128] = factor * jnp.sum(part_sum.T, axis=0, keepdims=True)

    for k in range(chunks):
        p_loads[k].wait()

    @pl.loop(0, chunks)
    def _(k):
        base = pl.multiple_of(k * chunk, chunk)
        for i in range(chunk // 128):
            p32 = protos[pl.ds(base + i * 128, 128), :].astype(jnp.float32)
            p32 = p32 * p32
            part_sum = sum(p32[:, 128 * n : 128 * n + 128] for n in range(width // 128))
            pn_line[0:1, pl.ds(base + i * 128, 128)] = factor * jnp.sum(part_sum.T, axis=0, keepdims=True)
        for i in range(chunk // 256):
            at = pl.ds(pl.multiple_of(base + i * 256, 256), 256)
            inner = dot(qall[0], protos[at, :], NT)
            logits[:, at] = inner * (2.0 * factor) - pn_line[0:1, at]

    pl.semaphore_wait(barrier, len(peers))

    half = queries // 2
    halves = (pl.ds(0, half), pl.ds(half, half))
    slot_at = {s: n for n, s in enumerate(SLOTS)}
    up, down = dev_pb(1, 0), dev_pb(NY - 1, 0)
    sibling = dev_pb(0, 1)

    def q_send(src_slot, dst_slot, rows, n, dev):
        sent.append(
            send(qall.at[src_slot, rows], qall.at[dst_slot, rows], q_ssem.at[n], q_rsem.at[n], dev)
        )

    q_send(0, slot_at[3, 0], halves[0], 0, up)
    q_send(0, slot_at[1, 0], halves[1], 2, down)
    q_send(0, slot_at[0, 1], halves[0], 6, sibling)
    q_send(0, slot_at[0, 1], halves[1], 7, sibling)
    q_send(0, slot_at[3, 0], halves[1], 1, up)
    q_send(0, slot_at[1, 0], halves[0], 3, down)

    def q_wait(slot, rows, n):
        arrived(qall.at[slot, rows], q_ssem.at[n], q_rsem.at[n])

    lane = lax.broadcasted_iota(jnp.int32, (16, 128), 1)

    @pl.loop(0, queries // 16)
    def _(r):
        rows = pl.ds(pl.multiple_of(r * 16, 16), 16)
        tiles = [logits[rows, 128 * k : 128 * k + 128] for k in range(classes // 128)]
        top = tiles[0]
        for t in tiles[1:]:
            top = jnp.maximum(top, t)
        top = jnp.broadcast_to(jnp.max(top, axis=1, keepdims=True), (16, 128))
        label = lab_col[rows, :] - lane
        total = jnp.zeros((16, 128), jnp.float32)
        mine = jnp.zeros((16, 128), jnp.float32)
        for k, t in enumerate(tiles):
            mine = mine + jnp.where(label == 128 * k, t, 0.0)
            e = jnp.exp(t - top)
            total = total + e
            logits[rows, 128 * k : 128 * k + 128] = e
        m_col[rows, :] = top
        tot_col[rows, :] = total
        lbl_col[rows, :] = mine

    q_line = row_line[1:2, :]
    m_line = m_col[...].T[0:1] - q_line
    t_line = jnp.sum(tot_col[...].T, axis=0, keepdims=True)
    l_line = jnp.sum(lbl_col[...].T, axis=0, keepdims=True)
    has = jnp.logical_and(my_label >= first_class, my_label < first_class + classes)
    l_line = jnp.where(has, l_line - q_line, 0.0)
    stat_x[x] = jnp.concatenate([rows_of(m_line + jnp.log(t_line)), rows_of(l_line)], axis=0)

    upper = lax.broadcasted_iota(jnp.int32, (8, 128), 0) < 4

    def combined(tiles):
        top = tiles[0]
        for t in tiles[1:]:
            top = jnp.maximum(top, t)
        total = sum(jnp.exp(t - top) for t in tiles)
        return jnp.where(upper, top + jnp.log(total), sum(tiles))

    for d in (2, 1, 3):
        sent.append(send(stat_x.at[x], stat_x.at[x], st_ssem.at[d], st_rsem.at[x], dev_x(d)))
    for d in (1, 3, 2):
        arrived(stat_x.at[at_x(d)], st_ssem.at[0], st_rsem.at[at_x(d)])
    stat_z[z] = combined([stat_x[k] for k in range(NX)])
    for d in (4, 3, 5, 2, 6, 1, 7):
        sent.append(send(stat_z.at[z], stat_z.at[z], st_ssem.at[NX + d], st_rsem.at[NX + z], dev_z(d)))
    for d in (1, 7, 2, 6, 3, 5, 4):
        arrived(stat_z.at[at_z(d)], st_ssem.at[0], st_rsem.at[NX + at_z(d)])
    stats = combined([stat_z[k] for k in range(NZ)])
    log_total = lanes_of(stats, 0)
    loss_out[...] = stats[0:4] - stats[4:8]

    mine_line = log_total + q_line
    row_line[pl.ds(0, 1), :] = mine_line
    qb = jnp.concatenate([rows_of(mine_line), rows_of(mine_line)], axis=0)
    stat_x[NX] = qb
    for s in range(1, 8):
        dy, other = SLOTS[s]
        dst = slot_at[(NY - dy) % NY, other]
        sent.append(
            send(stat_x.at[NX], stat_x.at[NX + dst], pb_ssem.at[s], pb_rsem.at[dst], dev_pb(dy, other))
        )

    w_col[...] = jnp.broadcast_to(jnp.exp(m_line - log_total), (128, queries)).T

    def grad_rows(r):
        rows = pl.ds(pl.multiple_of(r * 16, 16), 16)
        label = lab_col[rows, :] - lane
        w = w_col[rows, :]
        for k in range(classes // 128):
            g = logits[rows, 128 * k : 128 * k + 128] * w
            g = g - jnp.where(label == 128 * k, 1.0, 0.0)
            grad[rows, 128 * k : 128 * k + 128] = g.astype(jnp.bfloat16)

    for d in (1, 3, 2, 0):
        at = pl.multiple_of(at_x(d) * block, block)

        @pl.loop(0, block // 16)
        def _(r):
            grad_rows(at_x(d) * (block // 16) + r)

        @pl.loop(0, width // 256)
        def _(n):
            cols = pl.ds(pl.multiple_of(n * 256, 256), 256)
            v = dot(grad[pl.ds(at, block), :], protos[:, cols], NN)
            if d:
                for h in range(PARTS):
                    lines, power = coded(v[h * part : (h + 1) * part])
                    xs[d - 1, h, 0:part, cols] = lines
                    xs[d - 1, h, part : part + 16, cols] = power
            else:
                own_x[:, cols] = v

        if d:
            sent.append(send(xs.at[d - 1, 0], xr.at[d - 1, 0], x_ssem.at[d - 1, 0], x_rsem.at[d - 1, 0], dev_x(d)))
    for h in range(1, PARTS):
        for d in (1, 3, 2):
            sent.append(send(xs.at[d - 1, h], xr.at[d - 1, h], x_ssem.at[d - 1, h], x_rsem.at[d - 1, h], dev_x(d)))

    own_at = pl.multiple_of(pi * own_rows, own_rows)
    for i in range(own_rows // 128):
        p32 = protos[pl.ds(own_at + i * 128, 128), :].astype(jnp.float32)
        p32 = p32 * p32
        part_sum = sum(p32[:, 128 * n : 128 * n + 128] for n in range(width // 128))
        total = jnp.sum(part_sum, axis=1, keepdims=True) * factor
        pn_own[pl.ds(i * 128, 128), :] = jnp.broadcast_to(total, (128, 128))

    def proto_block(slot, first):
        pb = pb_of(slot)
        if slot:
            arrived(stat_x.at[NX + slot], pb_ssem.at[slot], pb_rsem.at[slot])
        term = lanes_of(stat_x[NX + slot], 0)
        label = lanes_of(labels[pb], 0) - first_class - own_at

        @pl.loop(0, own_rows // 128)
        def _(i):
            rows = pl.ds(pl.multiple_of(i * 128, 128), 128)
            inner = dot(protos[pl.ds(pl.multiple_of(own_at + i * 128, 128), 128), :], qall[slot], NT)
            pn = pn_own[rows, :]
            pn = jnp.concatenate([pn] * (queries // 128), axis=1)
            g = jnp.exp(inner * (2.0 * factor) - pn - term)
            index = lax.broadcasted_iota(jnp.int32, (128, queries), 0) + i * 128
            g = (g - jnp.where(index == label, 1.0, 0.0)).astype(jnp.bfloat16)
            g32 = g.astype(jnp.float32)
            col = sum(g32[:, 128 * n : 128 * n + 128] for n in range(queries // 128))
            for n in range(width // 512):
                cols = slice(512 * n, 512 * n + 512)
                moment = dot(g, qall[slot, :, cols], NN)
                if first:
                    acc[rows, cols] = moment
                else:
                    acc[rows, cols] += moment
            if first:
                coltot[rows, :] = col
            else:
                coltot[rows, :] += col

    def x_done(h):
        for d in (1, 3, 2):
            arrived(xr.at[d - 1, h], x_ssem.at[d - 1, h], x_rsem.at[d - 1, h])
        for n in range(NZ):
            cols = slice(128 * n, 128 * n + 128)
            v = own_x[h * part : (h + 1) * part, cols]
            for d in range(1, NX):
                s = scale_of(xr[d - 1, h, part : part + 16, cols])[0:1]
                v = v + xr[d - 1, h, 0:part, cols].astype(jnp.float32) * s
            own_x[h * part : (h + 1) * part, cols] = v
            lines, power = coded(v)
            zs[h, n, 0:part, :] = lines
            zs[h, n, part : part + 16, :] = power
        for d in (4, 3, 5, 2, 6, 1, 7):
            sent.append(
                send(zs.at[h, at_z(d)], zr.at[h, d], z_ssem.at[h, d], z_rsem.at[h, d], dev_z(d))
            )

    def z_done(h):
        for d in (1, 7, 2, 6, 3, 5, 4):
            arrived(zr.at[h, d], z_ssem.at[h, d], z_rsem.at[h, d])
        v = own_x[h * part : (h + 1) * part, pl.ds(pl.multiple_of(z * 128, 128), 128)]
        for d in range(1, NZ):
            s = scale_of(zr[h, d, part : part + 16, :])[0:1]
            v = v + zr[h, d, 0:part, :].astype(jnp.float32) * s
        lines, power = coded(v * (2.0 * factor))
        gx[h, x, z, 0:part, :] = lines
        gx[h, x, z, part : part + 16, :] = power
        for d in (4, 3, 5, 2, 6, 1, 7):
            sent.append(
                send(gx.at[h, x, z], gx.at[h, x, z], gz_ssem.at[h, d], gz_rsem.at[h, z], dev_z(d))
            )

    def gz_done(h):
        for d in (1, 7, 2, 6, 3, 5, 4):
            arrived(gx.at[h, x, at_z(d)], gz_ssem.at[h, d], gz_rsem.at[h, at_z(d)])
        for d in (2, 1, 3):
            sent.append(send(gx.at[h, x], gx.at[h, x], gx_ssem.at[h, d], gx_rsem.at[h, x], dev_x(d)))

    def write_rows(h, xq):
        at = pl.ds(pl.multiple_of(xq * block + h * part, part), part)
        for n in range(NZ):
            s = scale_of(gx[h, xq, n, part : part + 16, :])[0:1]
            qg_out[at, 128 * n : 128 * n + 128] = gx[h, xq, n, 0:part, :].astype(jnp.float32) * s

    def to_other_core(slot, first):
        dy = SLOTS[slot][0]
        for k in range(2):
            q_send(slot, slot_at[dy, 1], halves[k], first + k, sibling)

    def relay():
        q_wait(slot_at[3, 0], halves[0], 0)
        q_send(slot_at[3, 0], slot_at[2, 0], halves[0], 4, up)
        q_wait(slot_at[1, 0], halves[1], 2)
        q_send(slot_at[1, 0], slot_at[2, 0], halves[1], 5, down)

    proto_block(0, True)
    q_wait(slot_at[0, 1], halves[0], 6)
    q_wait(slot_at[0, 1], halves[1], 7)
    proto_block(1, False)
    relay()
    x_done(0)
    x_done(1)
    z_done(0)
    z_done(1)
    q_wait(slot_at[3, 0], halves[1], 1)
    to_other_core(2, 8)
    q_wait(slot_at[1, 0], halves[0], 3)
    to_other_core(3, 10)
    gz_done(0)
    gz_done(1)
    proto_block(2, False)
    proto_block(3, False)
    for k in range(2):
        q_wait(slot_at[3, 1], halves[k], 8 + k)
    proto_block(4, False)
    for k in range(2):
        q_wait(slot_at[1, 1], halves[k], 10 + k)
    proto_block(5, False)
    q_wait(slot_at[2, 0], halves[0], 4)
    q_wait(slot_at[2, 0], halves[1], 5)
    to_other_core(6, 12)
    proto_block(6, False)
    for k in range(2):
        q_wait(slot_at[2, 1], halves[k], 12 + k)
    proto_block(7, False)

    @pl.loop(0, own_rows // 128)
    def _(i):
        rows = pl.ds(pl.multiple_of(i * 128, 128), 128)
        own = protos[pl.ds(pl.multiple_of(own_at + i * 128, 128), 128), :].astype(jnp.float32)
        total = jnp.sum(coltot[rows, :], axis=1, keepdims=True)
        pg_out[rows, :] = (2.0 * factor) * (acc[rows, :] - total * own)

    for h in range(PARTS):
        write_rows(h, x)
    for h in range(PARTS):
        for d in (1, 3, 2):
            arrived(gx.at[h, at_x(d)], gx_ssem.at[h, d], gx_rsem.at[h, at_x(d)])
            write_rows(h, at_x(d))
    for copy in sent:
        copy.wait_send()


def local(queries, labels, prototypes):
    rows, width = queries.shape
    classes = prototypes.shape[0]
    own_rows = classes // (2 * NY)
    block = rows // NX
    part = block // PARTS
    vmem = pltpu.VMEM
    dma = pltpu.SemaphoreType.DMA
    f32, bf16, i16 = jnp.float32, jnp.bfloat16, jnp.int16
    scratch = [
        vmem((classes, width), bf16),
        vmem((2 * NY, rows, width), bf16),
        vmem((rows, classes), f32),
        vmem((rows, classes), bf16),
        vmem((8, classes), f32),
        vmem((block, width), f32),
        vmem((NX + 8, 8, 128), f32),
        vmem((NZ, 8, 128), f32),
        vmem((8, rows), f32),
        vmem((rows, 128), jnp.int32),
        vmem((rows, 128), f32),
        vmem((rows, 128), f32),
        vmem((rows, 128), f32),
        vmem((rows, 128), f32),
        vmem((NX - 1, PARTS, part + 16, width), i16),
        vmem((NX - 1, PARTS, part + 16, width), i16),
        vmem((PARTS, NZ, part + 16, 128), i16),
        vmem((PARTS, NZ, part + 16, 128), i16),
        vmem((part, 128), f32),
        vmem((PARTS, NX, NZ, part + 16, 128), i16),
        vmem((own_rows, width), f32),
        vmem((own_rows, 128), f32),
        vmem((own_rows, 128), f32),
        dma((classes // 512 + 1,)),
        dma((14,)), dma((14,)),
        dma((NX + NZ,)), dma((NX + NZ,)),
        dma((8,)), dma((8,)),
        dma((NX - 1, PARTS)), dma((NX - 1, PARTS)),
        dma((PARTS, NZ)), dma((PARTS, NZ)),
        dma((PARTS, NZ)), dma((PARTS, NZ)),
        dma((PARTS, NX)), dma((PARTS, NX)),
    ]
    loss, query_grad, proto_grad = pl.pallas_call(
        kernel,
        out_shape=(
            jax.ShapeDtypeStruct((4, rows // 4), f32),
            jax.ShapeDtypeStruct((rows, width), f32),
            jax.ShapeDtypeStruct((own_rows, width), f32),
        ),
        in_specs=[
            pl.BlockSpec(memory_space=pl.ANY),
            pl.BlockSpec(memory_space=pltpu.VMEM),
            pl.BlockSpec(memory_space=pl.ANY),
        ],
        out_specs=[pl.BlockSpec(memory_space=pltpu.VMEM)] * 3,
        scratch_shapes=scratch,
        compiler_params=pltpu.CompilerParams(
            collective_id=0, has_side_effects=True, vmem_limit_bytes=60 * 2**20
        ),
    )(queries, labels.reshape(2 * NY, 4, rows // 4), prototypes)
    return loss.reshape(rows), query_grad, proto_grad


def solution(mesh):
    placed = (P("pb", None), P(), P("cls", None))
    return jax.shard_map(
        local,
        mesh=mesh,
        in_specs=placed,
        out_specs=(P("pb"), P("pb", None), P(("cls", "pb"), None)),
        check_vma=False,
    )
```

time: 187 us -> 83 us (0.44)
  blocking collectives: 77.5 us -> 0 us
  Pallas kernels: 0 us -> 75.1 us
  waiting for transfers between devices: 48 us -> 0 us
  matrix products: 18.5 us -> 0 us
  between operations: 14.2 us -> 0.64 us
  other arithmetic: 12.6 us -> 0 us
  starting transfers between devices: 5.63 us -> 0 us
  local copies, waits for them, and re-layouts: 9.22 us -> 5.67 us
    all_to_all x2 -> x0, blocking collectives: 77.5 us -> none  [the longest x1 53.6 us: sum_at_owner(): lax.all_to_all(parts, axis, split_axis=0, concat_axis=0, tiled=True)]
    pallas_call x0 -> x1, Pallas kernels: none -> 75.1 us  [local(): pl.pallas_call(kernel, out_shape=(jax.ShapeDtypeStruct((4, rows // 4), f3...]
    all_to_all x1 -> x0, waiting for transfers between devices: 48 us -> none  [copy_for_each(): lax.all_to_all(jnp.broadcast_to(value[None], (size, *value.shape)), axis,...]
    dot_general x3 -> x0, matrix products: 18.5 us -> none  [the longest x1 7.01 us: local(): lax.dot_general(grad_logit, queries, (((0,), (0,)), ((), ())), preferred_...]
    reduce_sum x5 -> x0, other arithmetic: 10.4 us -> none  [the longest x1 4.16 us: local(): proto_norm = jnp.sum(proto_float * proto_float, axis=1)]
    all_to_all x1 -> x0, starting transfers between devices: 5.59 us -> none  [copy_for_each(): lax.all_to_all(jnp.broadcast_to(value[None], (size, *value.shape)), axis,...]
    unnamed x13 -> x5, local copies, waits for them, and re-layouts: 6.21 us -> 5.67 us
  transfers between devices with their start and end apart: 2 -> 0, of which waited for: 1 -> 0; matrix products, arithmetic and copies ran while one was open for 5% -> 0% of each run, Pallas kernels for 0% -> 0%
where the time goes in v1:
time: 83 us; the launch traced here: 81.4 us
  Pallas kernels  75.1 us (90%)
  local copies, waits for them, and re-layouts  5.67 us (7%)
    pallas_call x1, Pallas kernels, local(): pl.pallas_call(kernel, out_shape=(jax.ShapeDtypeStruct((4, rows // 4), f3...  75.1 us
    unnamed x5, local copies, waits for them, and re-layouts  5.67 us

profile of v1, /device:TPU:24, one launch (start us, length us, event | category | flops | bytes accessed | tf_op | source)
XLA Modules:
  0.0 81.4 jit_solution(16008729075135663419)
XLA Ops:
  0.6 75.1 %shard_map.58 = (f32[4,128]{1,0:T(4,128)}, f32[512,1024]{1,0:T(8,128)}, f32[384,1024]{1,0:T(8,128)}) custom-call(bf16[512,1024]{1,0:T(8,128)(2,1)} %q_in.1, s32[8,4,128]{2,1,0:T(4,128)} %bitcast.2, bf16[3072,1024]{1,0:T(8,128)(2,1)} %p_in.1), custom_call_target="tpu_custom_call" | custom-call | tf_op jit(solution)/shard_map/pallas_call | solution.py:445
  75.7 1.3 %copy.9 = f32[512]{0:T(512)} copy(f32[512]{0:T(512)} %bitcast.3) | data formatting | bytes 4096
  77.0 0.0 copy-start
  77.0 3.3 %copy.10 = f32[512,1024]{1,0:T(8,128)} copy(f32[512,1024]{1,0:T(8,128)} %get-tuple-element.13) | data formatting | bytes 4194304
  80.2 0.0 copy-done
  80.2 1.1 %copy.11 = f32[384,1024]{1,0:T(8,128)} copy(f32[384,1024]{1,0:T(8,128)S(1)} %copy-done) | data formatting | bytes 3145728
Async XLA Ops:
  77.0 3.3 %copy-start = (f32[384,1024]{1,0:T(8,128)S(1)}, f32[384,1024]{1,0:T(8,128)}, u32[]{:S(2)}) copy-start(f32[384,1024]{1,0:T(8,128)} %get-tuple-element.14) | copy-start | bytes 4718596

commit v2 on v1

v2 whole, which is shorter than its diff:
```python
import math

import jax
import jax.numpy as jnp
from jax import lax
from jax.experimental import pallas as pl
from jax.experimental.pallas import tpu as pltpu
from jax.sharding import PartitionSpec as P

MESH = pl.DeviceIdType.MESH
NX, NZ, NY = 4, 8, 4
PARTS = 2
TOP = 32000.0

NT = (((1,), (1,)), ((), ()))
NN = (((1,), (0,)), ((), ()))
SLOTS = ((0, 0), (0, 1), (3, 0), (1, 0), (3, 1), (1, 1), (2, 0), (2, 1))


def dot(a, b, dims):
    return lax.dot_general(a, b, dims, preferred_element_type=jnp.float32)


def coded(value):
    top = jnp.max(jnp.abs(value), axis=0, keepdims=True)
    power = jnp.ceil(jnp.log2(jnp.maximum(top, 1e-30)) + 1e-4)
    lines = jnp.round(value * (jnp.exp2(-power) * TOP))
    lines = jnp.clip(lines, -32767.0, 32767.0)
    return power, lines.astype(jnp.int32).astype(jnp.int16)


def rows16(power):
    return jnp.broadcast_to(power, (16, power.shape[1])).astype(jnp.int32).astype(jnp.int16)


def scale_of(power):
    return jnp.exp2(power.astype(jnp.float32)) * (1.0 / TOP)


def lanes_of(tile, first):
    return jnp.concatenate([tile[first + k : first + k + 1] for k in range(4)], axis=1)


def rows_of(line):
    return jnp.concatenate([line[:, 128 * k : 128 * k + 128] for k in range(4)], axis=0)


def kernel(
    q_in, labels, p_in, stat_out, gx, gsc, pg_out,
    protos, qall, raw, expo, grad, pn_line, own_x, stat, term, row_line,
    lab_col, top_col, tot_col, lbl_col,
    xs, xr, xsc, xrc, zs, zr, acc, coltot, pn_own, gbuf,
    in_sem, q_ssem, q_rsem, st_ssem, st_rsem, pb_ssem, pb_rsem,
    x_ssem, x_rsem, xc_ssem, xc_rsem, z_ssem, z_rsem, gz_ssem, gz_rsem,
    gx_ssem, gx_rsem, gc_ssem, gc_rsem,
):
    ci, pi = lax.axis_index("cls"), lax.axis_index("pb")
    z, x, y, core = ci // NX, lax.rem(ci, NX), pi // 2, lax.rem(pi, 2)
    queries, width = q_in.shape
    classes = p_in.shape[0]
    own_rows = pg_out.shape[0]
    factor = 1.0 / math.sqrt(width)
    block = queries // NX
    part = block // PARTS
    first_class = ci * classes

    def at_x(d):
        return lax.rem(x + d, NX)

    def at_z(d):
        return lax.rem(z + d, NZ)

    def dev_x(d):
        return (z * NX + at_x(d), pi)

    def dev_z(d):
        return (at_z(d) * NX + x, pi)

    def dev_pb(dy, other):
        return (ci, lax.rem(y + dy, NY) * 2 + lax.rem(core + other, 2))

    def pb_of(slot):
        dy, other = SLOTS[slot]
        return lax.rem(y + dy, NY) * 2 + lax.rem(core + other, 2)

    def send(src, dst, ssem, rsem, dev):
        copy = pltpu.make_async_remote_copy(
            src_ref=src, dst_ref=dst, send_sem=ssem, recv_sem=rsem, device_id=dev, device_id_type=MESH
        )
        copy.start()
        return copy

    def arrived(ref, ssem, rsem):
        pltpu.make_async_remote_copy(
            src_ref=ref, dst_ref=ref, send_sem=ssem, recv_sem=rsem, device_id=(ci, pi), device_id_type=MESH
        ).wait_recv()

    sent = []

    sub = 256
    chunk = 1024
    subs = chunk // sub
    chunks = classes // chunk
    q_load = pltpu.make_async_copy(q_in, qall.at[0], in_sem.at[classes // sub])
    q_load.start()

    def p_load(k):
        at = pl.ds(pl.multiple_of(k * sub, sub), sub)
        return pltpu.make_async_copy(p_in.at[at], protos.at[at], in_sem.at[k])

    for k in range(classes // sub):
        p_load(k).start()

    barrier = pltpu.get_barrier_semaphore()
    group = NX * NZ

    @pl.loop(1, group)
    def _(d):
        dev = (lax.rem(ci + d, group), pi)
        pl.semaphore_signal(barrier, inc=1, device_id=dev, device_id_type=MESH)

    for s in range(1, 2 * NY):
        pl.semaphore_signal(barrier, inc=1, device_id=dev_pb(*SLOTS[s]), device_id_type=MESH)

    q_load.wait()
    my_label = lanes_of(labels[pi], 0)
    lab_col[...] = jnp.broadcast_to(my_label - first_class, (128, queries)).T

    for k in range(queries // 128):
        q32 = qall[0, pl.ds(k * 128, 128), :].astype(jnp.float32)
        q32 = q32 * q32
        part_sum = sum(q32[:, 128 * i : 128 * i + 128] for i in range(width // 128))
        row_line[1:2, 128 * k : 128 * k + 128] = factor * jnp.sum(part_sum.T, axis=0, keepdims=True)

    half = queries // 2
    halves = (pl.ds(0, half), pl.ds(half, half))
    slot_at = {s: n for n, s in enumerate(SLOTS)}
    up, down = dev_pb(1, 0), dev_pb(NY - 1, 0)
    sibling = dev_pb(0, 1)

    def q_send(src_slot, dst_slot, rows, n, dev):
        sent.append(
            send(qall.at[src_slot, rows], qall.at[dst_slot, rows], q_ssem.at[n], q_rsem.at[n], dev)
        )

    def q_wait(slot, rows, n):
        arrived(qall.at[slot, rows], q_ssem.at[n], q_rsem.at[n])

    def start_queries():
        pl.semaphore_wait(barrier, group - 1 + 2 * NY - 1)
        q_send(0, slot_at[3, 0], halves[0], 0, up)
        q_send(0, slot_at[1, 0], halves[1], 2, down)
        q_send(0, slot_at[0, 1], halves[0], 6, sibling)
        q_send(0, slot_at[0, 1], halves[1], 7, sibling)
        q_send(0, slot_at[3, 0], halves[1], 1, up)
        q_send(0, slot_at[1, 0], halves[0], 3, down)


    lane = lax.broadcasted_iota(jnp.int32, (16, 128), 1)
    tiles = chunk // 128
    row_step = queries // subs

    def logits_of(k, n):
        p_load(k * subs + n).wait()
        base = pl.multiple_of(k * chunk + n * sub, sub)
        for i in range(sub // 128):
            p32 = protos[pl.ds(base + i * 128, 128), :].astype(jnp.float32)
            p32 = p32 * p32
            part_sum = sum(p32[:, 128 * m : 128 * m + 128] for m in range(width // 128))
            pn_line[0:1, pl.ds(base + i * 128, 128)] = factor * jnp.sum(part_sum.T, axis=0, keepdims=True)
        at = pl.ds(base, sub)
        inner = dot(qall[0], protos[at, :], NT)
        raw[k % 2][:, pl.ds(pl.multiple_of(n * sub, sub), sub)] = inner * (2.0 * factor) - pn_line[0:1, at]

    def exp_of(k, n):
        for r in range(row_step // 16):
            rows = pl.ds(pl.multiple_of(n * row_step + r * 16, 16), 16)
            line = [raw[k % 2][rows, 128 * t : 128 * t + 128] for t in range(tiles)]
            top = line[0]
            for t in line[1:]:
                top = jnp.maximum(top, t)
            label = lab_col[rows, :] - lane
            total = jnp.zeros((16, 128), jnp.float32)
            mine = lbl_col[rows, :] if k else jnp.zeros((16, 128), jnp.float32)
            for t, value in enumerate(line):
                mine = mine + jnp.where(label == k * chunk + 128 * t, value, 0.0)
                e = jnp.exp(value - top)
                total = total + e
                expo[k][rows, 128 * t : 128 * t + 128] = e
            top_col[k, rows, :] = top
            tot_col[k, rows, :] = total
            lbl_col[rows, :] = mine

    for k in range(chunks + 1):

        @pl.loop(0, subs)
        def _(n):
            if k < chunks:
                logits_of(k, n)
            if k:
                exp_of(k - 1, n)

        if k == 0:
            start_queries()

    q_line = row_line[1:2, :]
    top_all = top_col[0]
    for k in range(1, chunks):
        top_all = jnp.maximum(top_all, top_col[k])
    tot_all = sum(tot_col[k] * jnp.exp(top_col[k] - top_all) for k in range(chunks))
    top_all = top_all.T
    m_line = jnp.max(top_all, axis=0, keepdims=True)
    t_line = jnp.sum(tot_all.T * jnp.exp(top_all - m_line), axis=0, keepdims=True)
    l_line = jnp.sum(lbl_col[...].T, axis=0, keepdims=True)
    has = jnp.logical_and(my_label >= first_class, my_label < first_class + classes)
    l_line = jnp.where(has, l_line - q_line, 0.0)
    stat[ci] = jnp.concatenate([rows_of(m_line - q_line + jnp.log(t_line)), rows_of(l_line)], axis=0)

    @pl.loop(1, group)
    def _(d):
        dev = (lax.rem(ci + d, group), pi)
        send(stat.at[ci], stat.at[ci], st_ssem, st_rsem, dev)

    arrived(stat.at[pl.ds(0, group - 1)], st_ssem, st_rsem)
    top = stat[0]
    for k in range(1, group):
        top = jnp.maximum(top, stat[k])
    upper = lax.broadcasted_iota(jnp.int32, (8, 128), 0) < 4
    total = sum(jnp.exp(stat[k] - top) for k in range(group))
    stats = jnp.where(upper, top + jnp.log(total), sum(stat[k] for k in range(group)))
    stat_out[...] = stats
    log_total = lanes_of(stats, 0)

    mine_line = log_total + q_line
    term[0] = jnp.concatenate([rows_of(mine_line), rows_of(mine_line)], axis=0)
    shift = jnp.broadcast_to(mine_line, (128, queries)).T
    for k in range(chunks):
        top_col[k] = jnp.exp(top_col[k] - shift)

    def send_terms():
        for s in range(1, 2 * NY):
            dy, other = SLOTS[s]
            dst = slot_at[(NY - dy) % NY, other]
            sent.append(send(term.at[0], term.at[dst], pb_ssem.at[s], pb_rsem.at[dst], dev_pb(dy, other)))

    def grad_rows(r):
        rows = pl.ds(pl.multiple_of(r * 16, 16), 16)
        label = lab_col[rows, :] - lane
        for k in range(chunks):
            w = top_col[k, rows, :]
            for t in range(tiles):
                at = k * chunk + 128 * t
                g = expo[k][rows, 128 * t : 128 * t + 128] * w
                g = g - jnp.where(label == at, 1.0, 0.0)
                grad[rows, at : at + 128] = g.astype(jnp.bfloat16)

    def x_send(d, h):
        rows = pl.ds(h * part, part)
        at = d - 1
        sent.append(send(xs.at[at, rows], xr.at[at, rows], x_ssem.at[at, h], x_rsem.at[at, h], dev_x(d)))

    for d in (2, 1, 3, 0):
        at = pl.multiple_of(at_x(d) * block, block)

        @pl.loop(0, block // 16)
        def _(r):
            grad_rows(at_x(d) * (block // 16) + r)

        @pl.loop(0, width // 512)
        def _(n):
            cols = pl.ds(pl.multiple_of(n * 512, 512), 512)
            v = dot(grad[pl.ds(at, block), :], protos[:, cols], NN)
            if d:
                power, lines = coded(v)
                xs[d - 1, :, cols] = lines
                for m in range(4):
                    xsc[d - 1, pl.ds(n * 4 + m, 1), :] = scale_of(power[:, 128 * m : 128 * m + 128])
            else:
                own_x[:, cols] = v

        if d:
            sent.append(send(xsc.at[d - 1], xrc.at[d - 1], xc_ssem.at[d - 1], xc_rsem.at[d - 1], dev_x(d)))
            x_send(d, 0)
        if d == 3:
            for e in (2, 1, 3):
                for h in range(1, PARTS):
                    x_send(e, h)
            send_terms()

    own_at = pl.multiple_of(pi * own_rows, own_rows)
    for i in range(own_rows // 128):
        p32 = protos[pl.ds(own_at + i * 128, 128), :].astype(jnp.float32)
        p32 = p32 * p32
        part_sum = sum(p32[:, 128 * n : 128 * n + 128] for n in range(width // 128))
        total = jnp.sum(part_sum, axis=1, keepdims=True) * factor
        pn_own[pl.ds(i * 128, 128), :] = jnp.broadcast_to(total, (128, 128))

    def proto_block(slot):
        pb = pb_of(slot)
        if slot:
            arrived(term.at[slot], pb_ssem.at[slot], pb_rsem.at[slot])
        shift = lanes_of(term[slot], 0)
        label = lanes_of(labels[pb], 0) - first_class - own_at
        for n in range(queries // 256):
            at = slice(256 * n, 256 * n + 256)
            inner = dot(protos[pl.ds(own_at, own_rows), :], qall[slot, at, :], NT)
            pn = pn_own[...]
            pn = jnp.concatenate([pn, pn], axis=1)
            g = jnp.exp(inner * (2.0 * factor) - pn - shift[:, at])
            index = lax.broadcasted_iota(jnp.int32, (own_rows, 256), 0)
            g = (g - jnp.where(index == label[:, at], 1.0, 0.0)).astype(jnp.bfloat16)
            gbuf[:, at] = g
            g32 = g.astype(jnp.float32)
            col = g32[:, 0:128] + g32[:, 128:256]
            if slot or n:
                coltot[...] += col
            else:
                coltot[...] = col

        @pl.loop(0, width // 256)
        def _(n):
            cols = pl.ds(pl.multiple_of(n * 256, 256), 256)
            moment = dot(gbuf[...], qall[slot, :, cols], NN)
            if slot:
                acc[:, cols] += moment
            else:
                acc[:, cols] = moment

    def x_done(h):
        rows = pl.ds(h * part, part)
        for d in (1, 3, 2):
            if h == 0:
                arrived(xrc.at[d - 1], xc_ssem.at[d - 1], xc_rsem.at[d - 1])
            arrived(xr.at[d - 1, rows], x_ssem.at[d - 1, h], x_rsem.at[d - 1, h])
        for n in range(NZ):
            cols = slice(128 * n, 128 * n + 128)
            v = own_x[rows, cols]
            for d in range(1, NX):
                v = v + xr[d - 1, rows, cols].astype(jnp.float32) * xrc[d - 1, n : n + 1, :]
            own_x[rows, cols] = v
            power, lines = coded(v)
            zs[h, n, 0:part, :] = lines
            zs[h, n, part : part + 16, :] = rows16(power)
        for d in (4, 3, 5, 2, 6, 1, 7):
            sent.append(send(zs.at[h, at_z(d)], zr.at[h, d], z_ssem.at[h, d], z_rsem.at[h, d], dev_z(d)))

    def z_done(h):
        for d in (1, 7, 2, 6, 3, 5, 4):
            arrived(zr.at[h, d], z_ssem.at[h, d], z_rsem.at[h, d])
        v = own_x[pl.ds(h * part, part), pl.ds(pl.multiple_of(z * 128, 128), 128)]
        for d in range(1, NZ):
            s = scale_of(zr[h, d, part : part + 16, :])[0:1]
            v = v + zr[h, d, 0:part, :].astype(jnp.float32) * s
        power, lines = coded(v * (2.0 * factor))
        gx[h, x, z, 0:part, :] = lines
        gx[h, x, z, part : part + 16, :] = rows16(power)
        for d in (4, 3, 5, 2, 6, 1, 7):
            sent.append(send(gx.at[h, x, z], gx.at[h, x, z], gz_ssem.at[h, d], gz_rsem.at[h, z], dev_z(d)))

    def gz_done(h):
        for d in (1, 7, 2, 6, 3, 5, 4):
            arrived(gx.at[h, x, at_z(d)], gz_ssem.at[h, d], gz_rsem.at[h, at_z(d)])
        gsc[h, x] = jnp.concatenate(
            [scale_of(gx[h, x, n, part : part + 16, :])[0:1] for n in range(NZ)], axis=0
        )
        for d in (2, 1, 3):
            sent.append(send(gsc.at[h, x], gsc.at[h, x], gc_ssem.at[h, d], gc_rsem.at[h, x], dev_x(d)))
            lines = gx.at[h, x, pl.ds(0, NZ), pl.ds(0, part)]
            sent.append(send(lines, lines, gx_ssem.at[h, d], gx_rsem.at[h, x], dev_x(d)))

    def gx_done(h):
        for d in (1, 3, 2):
            k = at_x(d)
            arrived(gsc.at[h, k], gc_ssem.at[h, d], gc_rsem.at[h, k])
            arrived(gx.at[h, k, pl.ds(0, NZ), pl.ds(0, part)], gx_ssem.at[h, d], gx_rsem.at[h, k])

    def to_other_core(slot, first):
        dy = SLOTS[slot][0]
        for k in range(2):
            q_send(slot, slot_at[dy, 1], halves[k], first + k, sibling)

    def relay():
        q_wait(slot_at[3, 0], halves[0], 0)
        q_send(slot_at[3, 0], slot_at[2, 0], halves[0], 4, up)
        q_wait(slot_at[1, 0], halves[1], 2)
        q_send(slot_at[1, 0], slot_at[2, 0], halves[1], 5, down)

    proto_block(0)
    x_done(0)
    relay()
    q_wait(slot_at[0, 1], halves[0], 6)
    q_wait(slot_at[0, 1], halves[1], 7)
    proto_block(1)
    x_done(1)
    q_wait(slot_at[3, 0], halves[1], 1)
    to_other_core(2, 8)
    proto_block(2)
    z_done(0)
    q_wait(slot_at[1, 0], halves[0], 3)
    to_other_core(3, 10)
    proto_block(3)
    z_done(1)
    for k in range(2):
        q_wait(slot_at[3, 1], halves[k], 8 + k)
    proto_block(4)
    gz_done(0)
    for k in range(2):
        q_wait(slot_at[1, 1], halves[k], 10 + k)
    proto_block(5)
    gz_done(1)
    q_wait(slot_at[2, 0], halves[0], 4)
    q_wait(slot_at[2, 0], halves[1], 5)
    to_other_core(6, 12)
    proto_block(6)
    for k in range(2):
        q_wait(slot_at[2, 1], halves[k], 12 + k)
    proto_block(7)

    @pl.loop(0, own_rows // 128)
    def _(i):
        rows = pl.ds(pl.multiple_of(i * 128, 128), 128)
        own = protos[pl.ds(pl.multiple_of(own_at + i * 128, 128), 128), :].astype(jnp.float32)
        total = jnp.sum(coltot[rows, :], axis=1, keepdims=True)
        pg_out[rows, :] = (2.0 * factor) * (acc[rows, :] - total * own)

    for h in range(PARTS):
        gx_done(h)
    for copy in sent:
        copy.wait_send()
    pltpu.make_async_remote_copy(
        src_ref=stat.at[pl.ds(0, group - 1)], dst_ref=stat.at[pl.ds(0, group - 1)],
        send_sem=st_ssem, recv_sem=st_rsem, device_id=(ci, pi), device_id_type=MESH,
    ).wait_send()


def finish(stats, gx, gsc, pg, loss_out, qg_out, pg_out, loss, lines, sem):
    part = gx.shape[3] - 16
    block = PARTS * part
    copies = [pltpu.make_async_copy(pg, pg_out, sem.at[NX])]
    loss[...] = stats[0:4] - stats[4:8]
    copies.append(pltpu.make_async_copy(loss, loss_out, sem.at[NX + 1]))
    for copy in copies:
        copy.start()
    for k in range(NX):
        for h in range(PARTS):
            at = k * block + h * part
            for n in range(NZ):
                value = gx[h, k, n, 0:part, :].astype(jnp.float32) * gsc[h, k, n : n + 1, :]
                lines[at : at + part, 128 * n : 128 * n + 128] = value
        rows = pl.ds(k * block, block)
        copies.append(pltpu.make_async_copy(lines.at[rows], qg_out.at[rows], sem.at[k]))
        copies[-1].start()
    for copy in copies:
        copy.wait()


def local(queries, labels, prototypes):
    rows, width = queries.shape
    classes = prototypes.shape[0]
    own_rows = classes // (2 * NY)
    block = rows // NX
    part = block // PARTS
    vmem = pltpu.VMEM
    dma = pltpu.SemaphoreType.DMA
    f32, bf16, i16 = jnp.float32, jnp.bfloat16, jnp.int16
    sent_block = (PARTS, NX, NZ, part + 16, 128)
    scratch = [
        vmem((classes, width), bf16),
        vmem((2 * NY, rows, width), bf16),
        [vmem((rows, 1024), f32)] * 2,
        [vmem((rows, 1024), f32)] * (classes // 1024),
        vmem((rows, classes), bf16),
        vmem((8, classes), f32),
        vmem((block, width), f32),
        vmem((NX * NZ, 8, 128), f32),
        vmem((2 * NY, 8, 128), f32),
        vmem((8, rows), f32),
        vmem((rows, 128), jnp.int32),
        vmem((classes // 1024, rows, 128), f32),
        vmem((classes // 1024, rows, 128), f32),
        vmem((rows, 128), f32),
        vmem((NX - 1, block, width), i16),
        vmem((NX - 1, block, width), i16),
        vmem((NX - 1, 8, 128), f32),
        vmem((NX - 1, 8, 128), f32),
        vmem((PARTS, NZ, part + 16, 128), i16),
        vmem((PARTS, NZ, part + 16, 128), i16),
        vmem((own_rows, width), f32),
        vmem((own_rows, 128), f32),
        vmem((own_rows, 128), f32),
        vmem((own_rows, rows), bf16),
        dma((classes // 256 + 1,)),
        dma((14,)), dma((14,)),
        dma(()), dma(()),
        dma((8,)), dma((8,)),
        dma((NX - 1, PARTS)), dma((NX - 1, PARTS)),
        dma((NX - 1,)), dma((NX - 1,)),
        dma((PARTS, NZ)), dma((PARTS, NZ)),
        dma((PARTS, NZ)), dma((PARTS, NZ)),
        dma((PARTS, NX)), dma((PARTS, NX)),
        dma((PARTS, NX)), dma((PARTS, NX)),
    ]
    here = pl.BlockSpec(memory_space=pltpu.VMEM)
    anywhere = pl.BlockSpec(memory_space=pl.ANY)
    stats, gx, gsc, pg = pl.pallas_call(
        kernel,
        out_shape=(
            jax.ShapeDtypeStruct((8, 128), f32),
            jax.ShapeDtypeStruct(sent_block, i16),
            jax.ShapeDtypeStruct((PARTS, NX, NZ, 128), f32),
            jax.ShapeDtypeStruct((own_rows, width), f32),
        ),
        in_specs=[anywhere, here, anywhere],
        out_specs=[here] * 4,
        scratch_shapes=scratch,
        compiler_params=pltpu.CompilerParams(
            collective_id=0, has_side_effects=True, vmem_limit_bytes=48 * 2**20
        ),
    )(queries, labels.reshape(2 * NY, 4, rows // 4), prototypes)
    loss, query_grad, proto_grad = pl.pallas_call(
        finish,
        out_shape=(
            jax.ShapeDtypeStruct((4, rows // 4), f32),
            jax.ShapeDtypeStruct((rows, width), f32),
            jax.ShapeDtypeStruct((own_rows, width), f32),
        ),
        in_specs=[here] * 4,
        out_specs=[anywhere] * 3,
        scratch_shapes=[vmem((4, rows // 4), f32), vmem((rows, width), f32), dma((NX + 2,))],
        compiler_params=pltpu.CompilerParams(vmem_limit_bytes=8 * 2**20),
    )(stats, gx, gsc, pg)
    return loss.reshape(rows), query_grad, proto_grad


def solution(mesh):
    placed = (P("pb", None), P(), P("cls", None))
    return jax.shard_map(
        local,
        mesh=mesh,
        in_specs=placed,
        out_specs=(P("pb"), P("pb", None), P(("cls", "pb"), None)),
        check_vma=False,
    )
```

time: 83 us -> 65.7 us (0.79); the launches traced: 81.4 us -> 65.5 us
  Pallas kernels: 75.1 us -> 62.9 us
  local copies, waits for them, and re-layouts: 5.67 us -> 1.93 us
    pallas_call x1 -> x2, Pallas kernels: 75.1 us -> 62.9 us  [the longest x1 61 us: local(): pl.pallas_call(kernel, out_shape=(jax.ShapeDtypeStruct((8, 128), f32), ja...]
    unnamed x5 -> x4, local copies, waits for them, and re-layouts: 5.67 us -> 1.93 us
where the time goes in v2:
time: 65.7 us; the launch traced here: 65.5 us
  Pallas kernels  62.9 us (96%)
  local copies, waits for them, and re-layouts  1.93 us (3%)
    pallas_call x1, Pallas kernels, local(): pl.pallas_call(kernel, out_shape=(jax.ShapeDtypeStruct((8, 128), f32), ja...  61 us
    unnamed x4, local copies, waits for them, and re-layouts  1.93 us
    pallas_call x1, Pallas kernels, local(): pl.pallas_call(finish, out_shape=(jax.ShapeDtypeStruct((4, rows // 4), f3...  1.89 us

profile of v2, /device:TPU:24, one launch (start us, length us, event | category | flops | bytes accessed | tf_op | source)
XLA Modules:
  0.0 65.5 jit_solution(9546263423395918967)
XLA Ops:
  0.6 0.0 copy-start
  0.6 1.2 %copy-done = bf16[512,1024]{1,0:T(8,128)(2,1)S(1)} copy-done((bf16[512,1024]{1,0:T(8,128)(2,1)S(1)}, bf16[512,1024]{1,0:T(8,128)(2,1)}, u32[]{:S(2)}) %copy-start) | copy-done | bytes 1048600
  1.9 0.0 copy-start.1
  1.9 0.7 %copy-done.1 = s32[4096]{0:T(1024)S(1)} copy-done((s32[4096]{0:T(1024)S(1)}, s32[4096]{0:T(1024)}, u32[]{:S(2)}) %copy-start.1) | copy-done | bytes 16408
  2.6 61.0 %shard_map.58 = (f32[8,128]{1,0:T(8,128)S(1)}, s16[2,4,8,80,128]{4,3,2,1,0:T(8,128)(2,1)S(1)}, f32[2,4,8,128]{3,2,1,0:T(8,128)S(1)}, f32[384,1024]{1,0:T(8,128)S(1)}) custom-call(bf16[512,1024]{1,0:T(8,128)(2,1)S(1)} %copy-done, s32[8,4,128]{2,1,0:T(4,128)S(1)} %bitcast.2, bf16[3072,1024]{1,0:T(8,128)(2,1)} %p_in.1), custom_call_target="tpu_custom_call" | custom-call | tf_op jit(solution)/shard_map/pallas_call | solution.py:505
  63.6 1.9 %shard_map.59 = (f32[4,128]{1,0:T(4,128)}, f32[512,1024]{1,0:T(8,128)}, f32[384,1024]{1,0:T(8,128)}) custom-call(f32[8,128]{1,0:T(8,128)S(1)} %get-tuple-element.10.stats, s16[2,4,8,80,128]{4,3,2,1,0:T(8,128)(2,1)S(1)} %get-tuple-element.11.gx, f32[2,4,8,128]{3,2,1,0:T(8,128)S(1)} %get-tuple-element.12.gsc, f32[384,1024]{1,0:T(8,128)S(1)} %get-tuple-element.13.pg), custom_call_target="tpu_custom_call" | custom-call | tf_op jit(solution)/shard_map/pallas_call | solution.py:520
Async XLA Ops:
  0.6 1.2 %copy-start = (bf16[512,1024]{1,0:T(8,128)(2,1)S(1)}, bf16[512,1024]{1,0:T(8,128)(2,1)}, u32[]{:S(2)}) copy-start(bf16[512,1024]{1,0:T(8,128)(2,1)} %q_in.1) | copy-start | bytes 3145732
  1.9 0.7 %copy-start.1 = (s32[4096]{0:T(1024)S(1)}, s32[4096]{0:T(1024)}, u32[]{:S(2)}) copy-start(s32[4096]{0:T(1024)} %param.4) | copy-start | bytes 49156

commit v3 on v2

--- a/solution.py
+++ b/solution.py
@@ -46,10 +46,10 @@
 
 
 def kernel(
-    q_in, labels, p_in, stat_out, gx, gsc, pg_out,
-    protos, qall, raw, expo, grad, pn_line, own_x, stat, term, row_line,
+    q_in, labels_in, p_in, stat_out, gx, gsc, pg_out,
+    labels, protos, qall, raw, expo, grad, pn_line, own_x, stat, term, row_line,
     lab_col, top_col, tot_col, lbl_col,
-    xs, xr, xsc, xrc, zs, zr, acc, coltot, pn_own, gbuf,
+    xs, xr, xsc, xrc, zs, zr, acc, coltot, pn_own, gbuf, early,
     in_sem, q_ssem, q_rsem, st_ssem, st_rsem, pb_ssem, pb_rsem,
     x_ssem, x_rsem, xc_ssem, xc_rsem, z_ssem, z_rsem, gz_ssem, gz_rsem,
     gx_ssem, gx_rsem, gc_ssem, gc_rsem,
@@ -103,6 +103,8 @@
     chunks = classes // chunk
     q_load = pltpu.make_async_copy(q_in, qall.at[0], in_sem.at[classes // sub])
     q_load.start()
+    label_load = pltpu.make_async_copy(labels_in, labels, in_sem.at[classes // sub + 1])
+    label_load.start()
 
     def p_load(k):
         at = pl.ds(pl.multiple_of(k * sub, sub), sub)
@@ -122,10 +124,11 @@
     for s in range(1, 2 * NY):
         pl.semaphore_signal(barrier, inc=1, device_id=dev_pb(*SLOTS[s]), device_id_type=MESH)
 
-    q_load.wait()
+    label_load.wait()
     my_label = lanes_of(labels[pi], 0)
     lab_col[...] = jnp.broadcast_to(my_label - first_class, (128, queries)).T
 
+    q_load.wait()
     for k in range(queries // 128):
         q32 = qall[0, pl.ds(k * 128, 128), :].astype(jnp.float32)
         q32 = q32 * q32
@@ -147,7 +150,6 @@
         arrived(qall.at[slot, rows], q_ssem.at[n], q_rsem.at[n])
 
     def start_queries():
-        pl.semaphore_wait(barrier, group - 1 + 2 * NY - 1)
         q_send(0, slot_at[3, 0], halves[0], 0, up)
         q_send(0, slot_at[1, 0], halves[1], 2, down)
         q_send(0, slot_at[0, 1], halves[0], 6, sibling)
@@ -200,7 +202,8 @@
             if k:
                 exp_of(k - 1, n)
 
-        if k == 0:
+        if k == 1:
+            pl.semaphore_wait(barrier, group - 1 + 2 * NY - 1)
             start_queries()
 
     q_line = row_line[1:2, :]
@@ -221,6 +224,24 @@
         dev = (lax.rem(ci + d, group), pi)
         send(stat.at[ci], stat.at[ci], st_ssem, st_rsem, dev)
 
+    own_at = pl.multiple_of(pi * own_rows, own_rows)
+    for i in range(own_rows // 128):
+        p32 = protos[pl.ds(own_at + i * 128, 128), :].astype(jnp.float32)
+        p32 = p32 * p32
+        part_sum = sum(p32[:, 128 * n : 128 * n + 128] for n in range(width // 128))
+        total = jnp.sum(part_sum, axis=1, keepdims=True) * factor
+        pn_own[pl.ds(i * 128, 128), :] = jnp.broadcast_to(total, (128, 128))
+
+    for slot in range(2):
+        if slot:
+            for k in range(2):
+                q_wait(slot_at[0, 1], halves[k], 6 + k)
+
+        @pl.loop(0, queries // 256)
+        def _(n):
+            at = pl.ds(pl.multiple_of(n * 256, 256), 256)
+            early[slot, :, at] = dot(protos[pl.ds(own_at, own_rows), :], qall[slot, at, :], NT)
+
     arrived(stat.at[pl.ds(0, group - 1)], st_ssem, st_rsem)
     top = stat[0]
     for k in range(1, group):
@@ -257,18 +278,26 @@
     def x_send(d, h):
         rows = pl.ds(h * part, part)
         at = d - 1
-        sent.append(send(xs.at[at, rows], xr.at[at, rows], x_ssem.at[at, h], x_rsem.at[at, h], dev_x(d)))
-
-    for d in (2, 1, 3, 0):
+        return send(xs.at[at, rows], xr.at[at, rows], x_ssem.at[at, h], x_rsem.at[at, h], dev_x(d))
+
+    moving = {}
+    order = (2, 1, 3, 0)
+    steps = block // 16
+    turns = width // 512
+
+    @pl.loop(0, steps)
+    def _(r):
+        grad_rows(at_x(order[0]) * steps + r)
+
+    for i, d in enumerate(order):
         at = pl.multiple_of(at_x(d) * block, block)
 
-        @pl.loop(0, block // 16)
-        def _(r):
-            grad_rows(at_x(d) * (block // 16) + r)
-
-        @pl.loop(0, width // 512)
+        @pl.loop(0, turns)
         def _(n):
             cols = pl.ds(pl.multiple_of(n * 512, 512), 512)
+            if i + 1 < len(order):
+                for r in range(steps // turns):
+                    grad_rows(at_x(order[i + 1]) * steps + n * (steps // turns) + r)
             v = dot(grad[pl.ds(at, block), :], protos[:, cols], NN)
             if d:
                 power, lines = coded(v)
@@ -280,20 +309,14 @@
 
         if d:
             sent.append(send(xsc.at[d - 1], xrc.at[d - 1], xc_ssem.at[d - 1], xc_rsem.at[d - 1], dev_x(d)))
-            x_send(d, 0)
+            moving[d] = x_send(d, 0)
         if d == 3:
-            for e in (2, 1, 3):
-                for h in range(1, PARTS):
-                    x_send(e, h)
             send_terms()
-
-    own_at = pl.multiple_of(pi * own_rows, own_rows)
-    for i in range(own_rows // 128):
-        p32 = protos[pl.ds(own_at + i * 128, 128), :].astype(jnp.float32)
-        p32 = p32 * p32
-        part_sum = sum(p32[:, 128 * n : 128 * n + 128] for n in range(width // 128))
-        total = jnp.sum(part_sum, axis=1, keepdims=True) * factor
-        pn_own[pl.ds(i * 128, 128), :] = jnp.broadcast_to(total, (128, 128))
+            for h in range(1, PARTS):
+                for e in (2, 1, 3):
+                    sent.append(moving[e])
+                    moving[e] = x_send(e, h)
+    sent.extend(moving.values())
 
     def proto_block(slot):
         pb = pb_of(slot)
@@ -303,7 +326,10 @@
         label = lanes_of(labels[pb], 0) - first_class - own_at
         for n in range(queries // 256):
             at = slice(256 * n, 256 * n + 256)
-            inner = dot(protos[pl.ds(own_at, own_rows), :], qall[slot, at, :], NT)
+            if slot < 2:
+                inner = early[slot, :, at]
+            else:
+                inner = dot(protos[pl.ds(own_at, own_rows), :], qall[slot, at, :], NT)
             pn = pn_own[...]
             pn = jnp.concatenate([pn, pn], axis=1)
             g = jnp.exp(inner * (2.0 * factor) - pn - shift[:, at])
@@ -388,32 +414,30 @@
     proto_block(0)
     x_done(0)
     relay()
-    q_wait(slot_at[0, 1], halves[0], 6)
-    q_wait(slot_at[0, 1], halves[1], 7)
     proto_block(1)
     x_done(1)
     q_wait(slot_at[3, 0], halves[1], 1)
     to_other_core(2, 8)
-    proto_block(2)
-    z_done(0)
     q_wait(slot_at[1, 0], halves[0], 3)
     to_other_core(3, 10)
+    z_done(0)
+    proto_block(2)
+    z_done(1)
     proto_block(3)
-    z_done(1)
-    for k in range(2):
-        q_wait(slot_at[3, 1], halves[k], 8 + k)
+    gz_done(0)
+    q_wait(4, halves[0], 8)
+    q_wait(4, halves[1], 9)
     proto_block(4)
-    gz_done(0)
-    for k in range(2):
-        q_wait(slot_at[1, 1], halves[k], 10 + k)
+    gz_done(1)
+    q_wait(5, halves[0], 10)
+    q_wait(5, halves[1], 11)
     proto_block(5)
-    gz_done(1)
     q_wait(slot_at[2, 0], halves[0], 4)
     q_wait(slot_at[2, 0], halves[1], 5)
     to_other_core(6, 12)
     proto_block(6)
-    for k in range(2):
-        q_wait(slot_at[2, 1], halves[k], 12 + k)
+    q_wait(7, halves[0], 12)
+    q_wait(7, halves[1], 13)
     proto_block(7)
 
     @pl.loop(0, own_rows // 128)
@@ -423,9 +447,12 @@
         total = jnp.sum(coltot[rows, :], axis=1, keepdims=True)
         pg_out[rows, :] = (2.0 * factor) * (acc[rows, :] - total * own)
 
+    late = 2 * PARTS * (NX - 1)
+    for copy in sent[:-late]:
+        copy.wait_send()
     for h in range(PARTS):
         gx_done(h)
-    for copy in sent:
+    for copy in sent[-late:]:
         copy.wait_send()
     pltpu.make_async_remote_copy(
         src_ref=stat.at[pl.ds(0, group - 1)], dst_ref=stat.at[pl.ds(0, group - 1)],
@@ -465,6 +492,7 @@
     f32, bf16, i16 = jnp.float32, jnp.bfloat16, jnp.int16
     sent_block = (PARTS, NX, NZ, part + 16, 128)
     scratch = [
+        vmem((2 * NY, 4, rows // 4), jnp.int32),
         vmem((classes, width), bf16),
         vmem((2 * NY, rows, width), bf16),
         [vmem((rows, 1024), f32)] * 2,
@@ -489,7 +517,8 @@
         vmem((own_rows, 128), f32),
         vmem((own_rows, 128), f32),
         vmem((own_rows, rows), bf16),
-        dma((classes // 256 + 1,)),
+        vmem((2, own_rows, rows), f32),
+        dma((classes // 256 + 2,)),
         dma((14,)), dma((14,)),
         dma(()), dma(()),
         dma((8,)), dma((8,)),
@@ -510,7 +539,7 @@
             jax.ShapeDtypeStruct((PARTS, NX, NZ, 128), f32),
             jax.ShapeDtypeStruct((own_rows, width), f32),
         ),
-        in_specs=[anywhere, here, anywhere],
+        in_specs=[pl.BlockSpec(memory_space=pltpu.HBM)] * 3,
         out_specs=[here] * 4,
         scratch_shapes=scratch,
         compiler_params=pltpu.CompilerParams(

time: 65.7 us -> 64.4 us (0.980)
  Pallas kernels: 62.9 us -> 61.3 us
    pallas_call x1, Pallas kernels: 61 us -> 59.4 us  [local(): pl.pallas_call(kernel, out_shape=(jax.ShapeDtypeStruct((8, 128), f32), ja...]
where the time goes in v3:
time: 64.4 us; the launch traced here: 64 us
  Pallas kernels  61.3 us (95%)
  local copies, waits for them, and re-layouts  1.93 us (3%)
  between operations  0.81 us (1%)
    pallas_call x1, Pallas kernels, local(): pl.pallas_call(kernel, out_shape=(jax.ShapeDtypeStruct((8, 128), f32), ja...  59.4 us
    unnamed x4, local copies, waits for them, and re-layouts  1.93 us
    pallas_call x1, Pallas kernels, local(): pl.pallas_call(finish, out_shape=(jax.ShapeDtypeStruct((4, rows // 4), f3...  1.89 us

profile of v3, /device:TPU:24, one launch (start us, length us, event | category | flops | bytes accessed | tf_op | source)
XLA Modules:
  0.0 64.0 jit_solution(16070907877068822647)
XLA Ops:
  0.6 0.0 copy-start
  0.6 1.2 %copy-done = bf16[512,1024]{1,0:T(8,128)(2,1)S(1)} copy-done((bf16[512,1024]{1,0:T(8,128)(2,1)S(1)}, bf16[512,1024]{1,0:T(8,128)(2,1)}, u32[]{:S(2)}) %copy-start) | copy-done | bytes 1048600
  1.9 0.0 copy-start.1
  1.9 0.7 %copy-done.1 = s32[4096]{0:T(1024)S(1)} copy-done((s32[4096]{0:T(1024)S(1)}, s32[4096]{0:T(1024)}, u32[]{:S(2)}) %copy-start.1) | copy-done | bytes 16408
  2.6 59.4 %shard_map.58 = (f32[8,128]{1,0:T(8,128)S(1)}, s16[2,4,8,80,128]{4,3,2,1,0:T(8,128)(2,1)S(1)}, f32[2,4,8,128]{3,2,1,0:T(8,128)S(1)}, f32[384,1024]{1,0:T(8,128)S(1)}) custom-call(bf16[512,1024]{1,0:T(8,128)(2,1)S(1)} %copy-done, s32[8,4,128]{2,1,0:T(4,128)S(1)} %bitcast.2, bf16[3072,1024]{1,0:T(8,128)(2,1)} %p_in.1), custom_call_target="tpu_custom_call" | custom-call | tf_op jit(solution)/shard_map/pallas_call | solution.py:534
  62.0 1.9 %shard_map.59 = (f32[4,128]{1,0:T(4,128)}, f32[512,1024]{1,0:T(8,128)}, f32[384,1024]{1,0:T(8,128)}) custom-call(f32[8,128]{1,0:T(8,128)S(1)} %get-tuple-element.10.stats, s16[2,4,8,80,128]{4,3,2,1,0:T(8,128)(2,1)S(1)} %get-tuple-element.11.gx, f32[2,4,8,128]{3,2,1,0:T(8,128)S(1)} %get-tuple-element.12.gsc, f32[384,1024]{1,0:T(8,128)S(1)} %get-tuple-element.13.pg), custom_call_target="tpu_custom_call" | custom-call | tf_op jit(solution)/shard_map/pallas_call | solution.py:549
Async XLA Ops:
  0.6 1.2 %copy-start = (bf16[512,1024]{1,0:T(8,128)(2,1)S(1)}, bf16[512,1024]{1,0:T(8,128)(2,1)}, u32[]{:S(2)}) copy-start(bf16[512,1024]{1,0:T(8,128)(2,1)} %q_in.1) | copy-start | bytes 3145732
  1.9 0.7 %copy-start.1 = (s32[4096]{0:T(1024)S(1)}, s32[4096]{0:T(1024)}, u32[]{:S(2)}) copy-start(s32[4096]{0:T(1024)} %param.4) | copy-start | bytes 49156

commit v4 on v3

--- a/solution.py
+++ b/solution.py
@@ -281,7 +281,7 @@
         return send(xs.at[at, rows], xr.at[at, rows], x_ssem.at[at, h], x_rsem.at[at, h], dev_x(d))
 
     moving = {}
-    order = (2, 1, 3, 0)
+    order = (1, 3, 2, 0)
     steps = block // 16
     turns = width // 512
 
@@ -310,10 +310,10 @@
         if d:
             sent.append(send(xsc.at[d - 1], xrc.at[d - 1], xc_ssem.at[d - 1], xc_rsem.at[d - 1], dev_x(d)))
             moving[d] = x_send(d, 0)
-        if d == 3:
+        if d == 2:
             send_terms()
             for h in range(1, PARTS):
-                for e in (2, 1, 3):
+                for e in (1, 3, 2):
                     sent.append(moving[e])
                     moving[e] = x_send(e, h)
     sent.extend(moving.values())

time: 64.4 us -> 64.3 us (level)
  no operation moved by 1% of the time
where the time goes in v4:
time: 64.3 us; the launch traced here: 64.1 us
  Pallas kernels  61.3 us (95%)
  local copies, waits for them, and re-layouts  1.93 us (3%)
  between operations  0.81 us (1%)
    pallas_call x1, Pallas kernels, local(): pl.pallas_call(kernel, out_shape=(jax.ShapeDtypeStruct((8, 128), f32), ja...  59.5 us
    unnamed x4, local copies, waits for them, and re-layouts  1.93 us
    pallas_call x1, Pallas kernels, local(): pl.pallas_call(finish, out_shape=(jax.ShapeDtypeStruct((4, rows // 4), f3...  1.89 us

profile of v4, /device:TPU:24, one launch (start us, length us, event | category | flops | bytes accessed | tf_op | source)
XLA Modules:
  0.0 64.1 jit_solution(15861680449987611983)
XLA Ops:
  0.6 0.0 copy-start
  0.6 1.2 %copy-done = bf16[512,1024]{1,0:T(8,128)(2,1)S(1)} copy-done((bf16[512,1024]{1,0:T(8,128)(2,1)S(1)}, bf16[512,1024]{1,0:T(8,128)(2,1)}, u32[]{:S(2)}) %copy-start) | copy-done | bytes 1048600
  1.9 0.0 copy-start.1
  1.9 0.7 %copy-done.1 = s32[4096]{0:T(1024)S(1)} copy-done((s32[4096]{0:T(1024)S(1)}, s32[4096]{0:T(1024)}, u32[]{:S(2)}) %copy-start.1) | copy-done | bytes 16408
  2.6 59.5 %shard_map.58 = (f32[8,128]{1,0:T(8,128)S(1)}, s16[2,4,8,80,128]{4,3,2,1,0:T(8,128)(2,1)S(1)}, f32[2,4,8,128]{3,2,1,0:T(8,128)S(1)}, f32[384,1024]{1,0:T(8,128)S(1)}) custom-call(bf16[512,1024]{1,0:T(8,128)(2,1)S(1)} %copy-done, s32[8,4,128]{2,1,0:T(4,128)S(1)} %bitcast.2, bf16[3072,1024]{1,0:T(8,128)(2,1)} %p_in.1), custom_call_target="tpu_custom_call" | custom-call | tf_op jit(solution)/shard_map/pallas_call | solution.py:534
  62.0 1.9 %shard_map.59 = (f32[4,128]{1,0:T(4,128)}, f32[512,1024]{1,0:T(8,128)}, f32[384,1024]{1,0:T(8,128)}) custom-call(f32[8,128]{1,0:T(8,128)S(1)} %get-tuple-element.10.stats, s16[2,4,8,80,128]{4,3,2,1,0:T(8,128)(2,1)S(1)} %get-tuple-element.11.gx, f32[2,4,8,128]{3,2,1,0:T(8,128)S(1)} %get-tuple-element.12.gsc, f32[384,1024]{1,0:T(8,128)S(1)} %get-tuple-element.13.pg), custom_call_target="tpu_custom_call" | custom-call | tf_op jit(solution)/shard_map/pallas_call | solution.py:549
Async XLA Ops:
  0.6 1.2 %copy-start = (bf16[512,1024]{1,0:T(8,128)(2,1)S(1)}, bf16[512,1024]{1,0:T(8,128)(2,1)}, u32[]{:S(2)}) copy-start(bf16[512,1024]{1,0:T(8,128)(2,1)} %q_in.1) | copy-start | bytes 3145732
  1.9 0.7 %copy-start.1 = (s32[4096]{0:T(1024)S(1)}, s32[4096]{0:T(1024)}, u32[]{:S(2)}) copy-start(s32[4096]{0:T(1024)} %param.4) | copy-start | bytes 49156
